TPU v7x, 32 devices: a whole 2x2x4 slice. The times are simulated.
32 devices in a mesh: groups: 2 (over y), bond: 8 (over z, x), section: 2 (over core).
Axes of the slice: x: 2, y: 2, z: 4, core: 2. Of those that a mesh axis runs over, the one named last changes fastest.
Arguments:
- environment: float32 [2, 4096, 512], P(None, 'bond', 'groups'), parts along dimension 2, may hold values from -30 to 30
- outcomes: int32 [2, 2, 512], P('section', None, 'groups'), parts along dimension 2, may hold values from 0 to 3
- tensors: bfloat16 [2, 4, 4096, 4096], P('section', None, 'bond'), may hold values from -0.09375 to 0.09375
Outputs:
- section_envs: float32 [2, 2, 4096, 512], P('section', None, 'bond', 'groups'), parts along dimension 3
- log_scale: float32 [2, 2, 512], P('section', None, 'groups'), parts along dimension 2
There are 2 independent parts, one for each index of `groups`. A program takes and returns all parts, laid end to end along the dimension named above; an argument that names none is the same for every part. Nothing has to cross between parts.
All inputs are finite; a program needn't handle non-finite values.
Results may differ from a plain program's by a relative error of at most 0.0035.
Values may be sent and summed in bfloat16 or wider, within the bound.
A program may use at most 64 MiB of HBM per device.

v0:
```python
import functools
import math
import jax
import jax.numpy as jnp
from jax import lax
from jax.experimental import pallas as pl
from jax.experimental.pallas import tpu as pltpu
from jax.sharding import PartitionSpec as P

MESH = pl.DeviceIdType.MESH
LIFT = 1024.0
EPS = 1e-06
UNROLL = 8


def steps(start, stop, body):
    if stop - start <= UNROLL:
        for k in range(start, stop):
            body(k)
    else:
        def wrapped(k, carry):
            body(k)
            return carry
        lax.fori_loop(start, stop, wrapped, 0)


def outward(k, pos, size):
    near = jnp.minimum(pos, size - 1 - pos)
    half = (k + 1) // 2
    both = pos + jnp.where(k % 2 == 1, half, -half)
    single = jnp.where(pos <= size - 1 - pos, k, size - 1 - k)
    return jnp.where(k <= 2 * near, both, single)


def kernel(dims, codes_ref, env_ref, w_ref, prod_ref, factor_ref, log_ref,
           gathered, wbuf, envbuf, acc, passed, sums,
           env_sem, w_sem, out_sem, recv, own_x, own_z, pass_x, pass_z, relay, relay_z,
           sum_recv, sum_send):
    n, line, side, pieces, per_chunk, batches, outs, rows, cols = dims
    full_bond = n * rows
    me = lax.axis_index("bond")
    sec = lax.axis_index("section")
    my_z, my_x = me // side, me % side
    part = rows // pieces
    chunk_rows = per_chunk * rows
    chunks_row = side // per_chunk
    first = sec == 0

    def z_of(k):
        return outward(k, my_z, line)

    def x_of(k):
        return outward(k, my_x, side)

    def beside(k):
        return my_z + 2 * k - 1

    def on_line(z):
        return jnp.logical_and(z >= 0, z < line)

    def chunk_start(kz, kx):
        z = z_of(kz)
        return z * side + (x_of(kx) if per_chunk == 1 else 0)

    def piece(b, src, p):
        return gathered.at[b, src, pl.ds(p * part, part)]

    def send(src_ref, b, src, p, sem, bond, section):
        return pltpu.make_async_remote_copy(
            src_ref=src_ref, dst_ref=piece(b, src, p), send_sem=sem, recv_sem=recv.at[b, src, p],
            device_id={"bond": bond, "section": section}, device_id_type=MESH)

    def own_copy(b, p, k, along):
        if along == "x":
            return send(piece(b, me, p), b, me, p, own_x.at[b, k, p], my_z * side + x_of(k), 0)
        return send(piece(b, me, p), b, me, p, own_z.at[b, k, p], beside(k) * side + my_x, 0)

    def pass_copy(b, p, k, along):
        src = passed.at[b, pl.ds(p * part, part)]
        if along == "x":
            return send(src, b, me, p, pass_x.at[b, k, p], my_z * side + x_of(k), 1)
        return send(src, b, me, p, pass_z.at[b, k, p], beside(k) * side + my_x, 1)

    def relay_copy(b, p, kz, kx):
        src = z_of(kz) * side + my_x
        return send(piece(b, src, p), b, src, p, relay.at[b, kz, kx, p], my_z * side + x_of(kx), sec)

    def beyond(kz):
        return my_z + jnp.where(z_of(kz) < my_z, 1, -1)

    def relay_z_copy(b, p, kz):
        src = z_of(kz) * side + my_x
        return send(piece(b, src, p), b, src, p, relay_z.at[b, kz, p], beyond(kz) * side + my_x, sec)

    def relay_x(b, p, kz, act):
        steps(1, side, lambda kx: act(relay_copy(b, p, kz, kx)))

    def relay_line(b, p, kz, act):
        @pl.when(on_line(beyond(kz)))
        def _():
            act(relay_z_copy(b, p, kz))

    def both_sides(b, p, copy, act):
        for k in range(2):
            @pl.when(on_line(beside(k)))
            def _():
                act(copy(b, p, k, "z"))

    def start(copy):
        copy.start()

    def sent(copy):
        copy.wait_send()

    def await_piece(b, src, p):
        send(piece(b, src, p), b, src, p, own_x.at[b, 0, p], me, 1 - sec).wait_recv()

    def w_copy(kz, kx):
        at = pl.multiple_of(chunk_start(kz, kx) * rows, 128)
        return pltpu.make_async_copy(
            w_ref.at[:, :, pl.ds(at, chunk_rows)], wbuf.at[kz * chunks_row + kx], w_sem.at[kz * chunks_row + kx])

    def env_copy(b):
        return pltpu.make_async_copy(env_ref.at[b], envbuf.at[b], env_sem.at[b])

    def out_copy(b):
        return pltpu.make_async_copy(acc.at[b], prod_ref.at[b], out_sem.at[b])

    @pl.when(first)
    def _():
        for b in range(batches):
            env_copy(b).start()

    def start_w():
        def row_w(kz):
            for kx in range(chunks_row):
                w_copy(kz, kx).start()
        steps(0, line, row_w)

    pl.when(jnp.logical_not(first))(start_w)

    barrier = pltpu.get_barrier_semaphore()

    def neighbours(act):
        act(None, {"bond": me, "section": 1 - sec})
        for k in range(1, side):
            for section in range(2):
                act(None, {"bond": my_z * side + x_of(k), "section": section})
        for k in range(2):
            for section in range(2):
                act(on_line(beside(k)), {"bond": beside(k) * side + my_x, "section": section})

    def greet(there, who):
        def signal():
            pl.semaphore_signal(barrier, inc=1, device_id=who, device_id_type=MESH)
        signal() if there is None else pl.when(there)(signal)

    neighbours(greet)

    @pl.when(first)
    def _():
        for b in range(batches):
            env_copy(b).wait()
            gathered[b, me] = envbuf[b].astype(jnp.bfloat16)
    ends = jnp.where(my_z == 0, 1, 0) + jnp.where(my_z == line - 1, 1, 0)
    pl.semaphore_wait(barrier, 1 + 2 * (side - 1) + 2 * (2 - ends))

    def own_sends(b):
        for p in range(pieces):
            both_sides(b, p, own_copy, start)
            steps(1, side, lambda k: own_copy(b, p, k, "x").start())

    @pl.when(first)
    def _():
        own_sends(0)
        start_w()

    def forward(b, kz):
        src = z_of(kz) * side + my_x
        for p in range(pieces):
            await_piece(b, src, p)
            relay_line(b, p, kz, start)
            relay_x(b, p, kz, start)

    def await_shard(b, kz, kx):
        for p in range(pieces):
            await_piece(b, z_of(kz) * side + x_of(kx), p)

    def multiply(b, kz, kx, fresh):
        if b == 0:
            w_copy(kz, kx).wait()
        base = chunk_start(kz, kx)
        if per_chunk == 1:
            value = gathered[b, base]
        else:
            value = gathered[b, pl.ds(base, per_chunk)].reshape(chunk_rows, cols)
        at = kz * chunks_row + kx
        total = None
        for o in range(outs):
            chosen = jnp.where(codes_ref[pl.ds(b, 1), :] == o, 1.0, 0.0).astype(jnp.bfloat16)
            term = jnp.dot(wbuf[at, o], value * chosen, preferred_element_type=jnp.float32)
            total = term if total is None else total + term
        if fresh:
            acc[b] = total
        else:
            acc[b] += total

    def sum_copy(kind, b, o, section):
        peer = lax.rem(me + o, n)
        return pltpu.make_async_remote_copy(
            src_ref=sums.at[kind, b, me], dst_ref=sums.at[kind, b, me],
            send_sem=sum_send.at[section, b, o], recv_sem=sum_recv.at[kind, b, me],
            device_id={"bond": peer, "section": section}, device_id_type=MESH)

    def await_sum(kind, b, src):
        pltpu.make_async_remote_copy(
            src_ref=sums.at[kind, b, src], dst_ref=sums.at[kind, b, src],
            send_sem=sum_send.at[0, b, 0], recv_sem=sum_recv.at[kind, b, src],
            device_id={"bond": me, "section": 1 - sec}, device_id_type=MESH).wait_recv()

    def row(b, kz):
        fresh = isinstance(kz, int) and kz == 0
        if per_chunk == 1:
            for kx in range(side):
                if kx > 0 and not fresh:
                    await_shard(b, kz, kx)
                multiply(b, kz, kx, fresh and kx == 0)
        else:
            if not fresh:
                steps(1, side, lambda kx: await_shard(b, kz, kx))
            multiply(b, kz, 0, fresh)

    def await_own(b):
        @pl.when(jnp.logical_not(first))
        def _():
            for p in range(pieces):
                await_piece(b, me, p)

    def own_column(b, kz):
        multiply(b, kz, 0, isinstance(kz, int) and kz == 0)

    def other_columns(b, kz):
        for kx in range(1, side):
            await_shard(b, kz, kx)
            multiply(b, kz, kx, False)

    def next_own(b):
        if b + 1 < batches:
            @pl.when(first)
            def _():
                own_sends(b + 1)

    def next_forward(b):
        if b + 1 < batches and line > 1:
            forward(b + 1, 1)

    for b in range(batches):
        if line > 1 and b == 0:
            forward(b, 1)
        await_own(b)
        if per_chunk == 1 and line <= UNROLL:
            own_column(b, 0)
            for kz in range(2, line):
                forward(b, kz)
                if kz == line - 1:
                    next_own(b)
                other_columns(b, kz - 2)
                own_column(b, kz - 1)
            if line <= 2:
                next_own(b)
            for kz in range(max(line - 2, 0), line):
                if kz > 0 and kz == line - 1:
                    own_column(b, kz)
                    next_forward(b)
                other_columns(b, kz)
        else:
            steps(1, side, lambda kx: await_shard(b, 0, kx))
            steps(2, line, lambda kz: forward(b, kz))
            next_own(b)
            row(b, 0)
            steps(1, line - 1, lambda kz: row(b, kz))
            if line > 1:
                next_forward(b)
                row(b, line - 1)

        product = acc[b]

        @pl.when(first)
        def _():
            passed[b] = (product * LIFT).astype(jnp.bfloat16)
            for p in range(pieces):
                pass_copy(b, p, 0, "x").start()
                steps(1, side, lambda k: pass_copy(b, p, k, "x").start())
                both_sides(b, p, pass_copy, start)

        squares = jnp.sum(product * product, axis=0, keepdims=True)

        @pl.when(first)
        def _():
            sums[0, b, me] = squares
            steps(1, n, lambda o: sum_copy(0, b, o, 0).start())
            steps(0, n, lambda o: sum_copy(0, b, o, 1).start())

        @pl.when(jnp.logical_not(first))
        def _():
            sums[1, b, me] = squares
            steps(1, n, lambda o: sum_copy(1, b, o, 1).start())
        out_copy(b).start()

    def total_of(kind, b, own):
        steps(0 if not own else 1, n, lambda o: await_sum(kind, b, lax.rem(me + o, n)))
        return jnp.sum(sums[kind, b], axis=0)

    @pl.when(first)
    def _():
        for b in range(batches):
            scale = jnp.sqrt(total_of(0, b, True) / full_bond + EPS)
            factor_ref[pl.ds(b, 1), :] = 1.0 / scale
            log_ref[pl.ds(b, 1), :] = jnp.log(scale)

    @pl.when(jnp.logical_not(first))
    def _():
        for b in range(batches):
            before = jnp.sqrt(total_of(0, b, False) / full_bond + EPS)
            inner = 1.0 / (before * LIFT)
            scale = jnp.sqrt(total_of(1, b, True) * (inner * inner) / full_bond + EPS)
            factor_ref[pl.ds(b, 1), :] = inner / scale
            log_ref[pl.ds(b, 1), :] = jnp.log(before) + jnp.log(scale)

    for b in range(batches):
        out_copy(b).wait()
        for p in range(pieces):
            def drain(kz):
                relay_x(b, p, kz, sent)
                relay_line(b, p, kz, sent)
            steps(1, line, drain)

        @pl.when(first)
        def _():
            for p in range(pieces):
                steps(1, side, lambda k: own_copy(b, p, k, "x").wait_send())
                both_sides(b, p, own_copy, sent)
                steps(0, side, lambda k: pass_copy(b, p, k, "x").wait_send())
                both_sides(b, p, pass_copy, sent)
            steps(1, n, lambda o: sum_copy(0, b, o, 0).wait_send())
            steps(0, n, lambda o: sum_copy(0, b, o, 1).wait_send())

        @pl.when(jnp.logical_not(first))
        def _():
            steps(1, n, lambda o: sum_copy(1, b, o, 1).wait_send())


def side_of(n):
    side = math.isqrt(n // 2) if n > 1 else 1
    return side if side > 0 and n % side == 0 else 1


def shards(environment, outcomes, tensors):
    n = lax.axis_size("bond")
    batches, rows, cols = environment.shape
    outs = tensors.shape[1]
    side = side_of(n)
    line = n // side
    pieces = 2 if rows % 32 == 0 and rows >= 128 else 1
    per_chunk = 1 if rows % 128 == 0 else side
    n_chunks = n // per_chunk
    dims = (n, line, side, pieces, per_chunk, batches, outs, rows, cols)
    dma = pltpu.SemaphoreType.DMA
    vmem = pl.BlockSpec(memory_space=pltpu.VMEM)
    hbm = pl.BlockSpec(memory_space=pltpu.HBM)
    prod, factor, logs = pl.pallas_call(
        functools.partial(kernel, dims),
        out_shape=(
            jax.ShapeDtypeStruct((batches, rows, cols), jnp.float32),
            jax.ShapeDtypeStruct((batches, cols), jnp.float32),
            jax.ShapeDtypeStruct((batches, cols), jnp.float32),
        ),
        in_specs=[vmem, hbm, hbm],
        out_specs=(hbm, vmem, vmem),
        scratch_shapes=[
            pltpu.VMEM((batches, n, rows, cols), jnp.bfloat16),
            pltpu.VMEM((n_chunks, outs, rows, per_chunk * rows), jnp.bfloat16),
            pltpu.VMEM((batches, rows, cols), jnp.float32),
            pltpu.VMEM((batches, rows, cols), jnp.float32),
            pltpu.VMEM((batches, rows, cols), jnp.bfloat16),
            pltpu.VMEM((2, batches, n, 1, cols), jnp.float32),
            dma((batches,)),
            dma((n_chunks,)),
            dma((batches,)),
            dma((batches, n, pieces)),
            dma((batches, side, pieces)),
            dma((batches, 2, pieces)),
            dma((batches, side, pieces)),
            dma((batches, 2, pieces)),
            dma((batches, line, side, pieces)),
            dma((batches, line, pieces)),
            dma((2, batches, n)),
            dma((2, batches, n)),
        ],
        compiler_params=pltpu.CompilerParams(
            collective_id=0, has_side_effects=True, vmem_limit_bytes=56 * 2**20),
    )(outcomes[0], environment, tensors[0])
    return (prod * factor[:, None, :])[None], logs[None]


def solution(mesh):
    return jax.shard_map(
        shards,
        mesh=mesh,
        in_specs=(
            P(None, "bond", "groups"),
            P("section", None, "groups"),
            P("section", None, "bond", None),
        ),
        out_specs=(P("section", None, "bond", "groups"), P("section", None, "groups")),
        check_vma=False,
    )
```

profile of v0, /device:TPU:1, one launch (start us, length us, event | category | flops | bytes accessed | tf_op | source)
XLA Modules:
  0.0 78.3 jit_solution(8770775029599603394)
XLA Ops:
  0.6 74.2 %shard_map.50 = (f32[2,512,256]{2,1,0:T(8,128)}, f32[2,256]{1,0:T(2,128)}, f32[2,256]{1,0:T(2,128)}) custom-call(s32[2,256]{1,0:T(2,128)} %bitcast.6, f32[2,512,256]{2,1,0:T(8,128)} %env_ref.1, bf16[4,512,4096]{2,1,0:T(8,128)(2,1)} %bitcast.5), custom_call_target="tpu_custom_call" | custom-call | tf_op jit(solution)/shard_map/pallas_call | solution.py:371
  74.8 2.3 %multiply_bitcast_fusion = f32[1,2,512,256]{3,2,1,0:T(8,128)} fusion(f32[2,512,256]{2,1,0:T(8,128)} %get-tuple-element.5, f32[2,256]{1,0:T(2,128)} %get-tuple-element.6), kind=kLoop, calls=%fused_computation | loop fusion | flops 262144 | bytes 2099200 | tf_op jit(solution)/shard_map/broadcast_in_dim | solution.py:403
  77.1 1.2 %copy.6 = f32[1,2,256]{2,1,0:T(2,128)} copy(f32[1,2,256]{2,1,0:T(2,128)} %bitcast.7) | data formatting | bytes 4096
where the time goes:
time: 78.5 us; the launch traced here: 78.3 us
  Pallas kernels  74.2 us (95%)
  other arithmetic  2.27 us (3%)
  local copies, waits for them, and re-layouts  1.23 us (2%)
    pallas_call x1, Pallas kernels, shards(): pl.pallas_call(functools.partial(kernel, dims), out_shape=(jax.ShapeDtype...  74.2 us
    broadcast_in_dim x1, other arithmetic, shards(): return ((prod * factor[:, None, :])[None], logs[None])  2.27 us

commit v1 on v0

--- a/solution.py
+++ b/solution.py
@@ -350,6 +350,320 @@
             steps(1, n, lambda o: sum_copy(1, b, o, 1).wait_send())
 
 
+def pair_kernel(dims, codes_ref, env_ref, w_ref, prod_ref, factor_ref, log_ref,
+                gathered, wbuf, envbuf, acc, passed, sums,
+                env_sem, w_sem, out_sem, recv, own_sem, pass_sem, relay_sem, onward_sem, swap_sem,
+                sum_recv, sum_send):
+    n, line, batches, outs, rows, cols = dims
+    side, pieces = 2, 4
+    part, span = rows // pieces, rows // 2
+    me = lax.axis_index("bond")
+    sec = lax.axis_index("section")
+    my_z, my_x = me // side, me % side
+    first = sec == 0
+
+    low = my_z < line // 2
+    inner = jnp.logical_and(my_z > 0, my_z < line - 1)
+    rows_near = (my_z, my_z + 1 - 2 * (my_z % 2), jnp.where(low, 2, 1), jnp.where(low, 3, 0))
+
+    def row_of(k):
+        return rows_near[k]
+
+    def column(k):
+        return row_of(k) * side + my_x
+
+    def across(k):
+        return row_of(k) * side + 1 - my_x
+
+    blocks = [(me, half) for half in range(2)]
+    blocks += [(column(k), half) for half in range(2) for k in range(1, line)]
+    blocks += [(across(k), half) for half in range(2) for k in range(line)]
+
+    def column_slot(k, half):
+        return 2 + half * (line - 1) + k - 1
+
+    def across_slot(k, half):
+        return 2 * line + half * line + k
+
+    def piece(b, src, p):
+        return gathered.at[b, src, pl.ds(p * part, part)]
+
+    def send(src_ref, b, src, p, sem, bond, section):
+        return pltpu.make_async_remote_copy(
+            src_ref=src_ref, dst_ref=piece(b, src, p), send_sem=sem, recv_sem=recv.at[b, src, p],
+            device_id={"bond": bond, "section": section}, device_id_type=MESH)
+
+    def own_copy(b, p, k):
+        return send(piece(b, me, p), b, me, p, own_sem.at[b, k, p], across(0) if k == 0 else column(k), 0)
+
+    def pass_copy(b, p, k):
+        src = passed.at[b, pl.ds(p * part, part)]
+        bond = me if k == line else across(0) if k == 0 else column(k)
+        return send(src, b, me, p, pass_sem.at[b, k, p], bond, 1)
+
+    def relay_copy(b, k, p):
+        return send(piece(b, column(k), p), b, column(k), p, relay_sem.at[b, k, p], across(0), sec)
+
+    def onward_copy(b, p):
+        return send(piece(b, column(3), p), b, column(3), p, onward_sem.at[b, p], column(1), sec)
+
+    def swap_copy(b, p):
+        return send(piece(b, across(0), p), b, across(0), p, swap_sem.at[b, p], column(1), sec)
+
+    def direct(copy, b, p, k, act):
+        if k == 3:
+            pl.when(inner)(lambda: act(copy(b, p, k)))
+        else:
+            act(copy(b, p, k))
+
+    def start(copy):
+        copy.start()
+
+    def sent(copy):
+        copy.wait_send()
+
+    def await_piece(b, src, p):
+        send(piece(b, src, p), b, src, p, own_sem.at[b, 0, 0], me, 1 - sec).wait_recv()
+
+    def w_copies(slot):
+        src, half = blocks[slot]
+        at = pl.multiple_of(src * rows + half * span, 128)
+        return [pltpu.make_async_copy(
+            w_ref.at[o, :, pl.ds(at, span)], wbuf.at[slot, :, pl.ds(o * span, span)],
+            w_sem.at[slot, o]) for o in range(outs)]
+
+    def start_w():
+        for slot in range(2 * n):
+            for copy in w_copies(slot):
+                copy.start()
+
+    def env_copy(b):
+        return pltpu.make_async_copy(env_ref.at[b], envbuf.at[b], env_sem.at[b])
+
+    def out_copy(b):
+        return pltpu.make_async_copy(acc.at[b], prod_ref.at[b], out_sem.at[b])
+
+    @pl.when(first)
+    def _():
+        for b in range(batches):
+            env_copy(b).start()
+
+    pl.when(jnp.logical_not(first))(start_w)
+
+    barrier = pltpu.get_barrier_semaphore()
+
+    def greet(who):
+        pl.semaphore_signal(barrier, inc=1, device_id=who, device_id_type=MESH)
+
+    greet({"bond": me, "section": 1 - sec})
+    for section in range(2):
+        greet({"bond": across(0), "section": section})
+        for k in range(1, line):
+            greet({"bond": column(k), "section": section})
+
+    @pl.when(first)
+    def _():
+        env_copy(0).wait()
+        gathered[0, me] = envbuf[0].astype(jnp.bfloat16)
+
+    pl.semaphore_wait(barrier, 2 * line + 1)
+
+    def column_sends(b):
+        for p in range(pieces):
+            for k in range(1, line):
+                direct(own_copy, b, p, k, start)
+            if b == 0:
+                own_copy(b, p, 0).start()
+
+    @pl.when(first)
+    def _():
+        column_sends(0)
+        start_w()
+        for b in range(1, batches):
+            env_copy(b).wait()
+            gathered[b, me] = envbuf[b].astype(jnp.bfloat16)
+            column_sends(b)
+
+    def across_sends(b):
+        if b < batches:
+            @pl.when(first)
+            def _():
+                for p in range(pieces):
+                    own_copy(b, p, 0).start()
+
+    def forward(b, k, half):
+        for p in range(2 * half, 2 * half + 2):
+            await_piece(b, column(k), p)
+            if k == 3:
+                pl.when(inner)(lambda: onward_copy(b, p).start())
+            if k > 1 or half == 0:
+                relay_copy(b, k, p).start()
+
+    def arrived(b, k, half):
+        for p in range(2 * half, 2 * half + 2):
+            await_piece(b, across(k), p)
+            if k == 0 and half == 1:
+                swap_copy(b, p).start()
+        multiply(b, across_slot(k, half))
+
+    def multiply(b, slot):
+        src, half = blocks[slot]
+        if b == 0:
+            for copy in w_copies(slot):
+                copy.wait()
+        value = gathered[b, src, pl.ds(half * span, span)]
+        chosen = [jnp.where(codes_ref[pl.ds(b, 1), :] == o, 1.0, 0.0).astype(jnp.bfloat16) for o in range(outs)]
+        stacked = jnp.concatenate([value * c for c in chosen], axis=0)
+        term = jnp.dot(wbuf[slot], stacked, preferred_element_type=jnp.float32)
+        if slot == 0:
+            acc[b] = term
+        else:
+            acc[b] += term
+
+    def sum_copy(kind, b, o, section):
+        peer = lax.rem(me + o, n)
+        return pltpu.make_async_remote_copy(
+            src_ref=sums.at[kind, b, me], dst_ref=sums.at[kind, b, me],
+            send_sem=sum_send.at[section, b, o], recv_sem=sum_recv.at[kind, b, me],
+            device_id={"bond": peer, "section": section}, device_id_type=MESH)
+
+    def await_sum(kind, b, src):
+        pltpu.make_async_remote_copy(
+            src_ref=sums.at[kind, b, src], dst_ref=sums.at[kind, b, src],
+            send_sem=sum_send.at[0, b, 0], recv_sem=sum_recv.at[kind, b, src],
+            device_id={"bond": me, "section": 1 - sec}, device_id_type=MESH).wait_recv()
+
+    for b in range(batches):
+        forward(b, 1, 0)
+        @pl.when(jnp.logical_not(first))
+        def _():
+            for p in range(pieces):
+                await_piece(b, me, p)
+        multiply(b, 0)
+        multiply(b, 1)
+        forward(b, 2, 0)
+        multiply(b, column_slot(1, 0))
+        multiply(b, column_slot(2, 0))
+        arrived(b, 0, 0)
+        arrived(b, 0, 1)
+        forward(b, 3, 0)
+        multiply(b, column_slot(3, 0))
+        for k in range(1, line):
+            forward(b, k, 1)
+            multiply(b, column_slot(k, 1))
+        across_sends(b + 1)
+        for half in range(2):
+            for k in range(1, line):
+                arrived(b, k, half)
+
+        @pl.when(first)
+        def _():
+            for p in range(pieces):
+                at = pl.ds(p * part, part)
+                passed[b, at] = (acc[b, at] * LIFT).astype(jnp.bfloat16)
+                pass_copy(b, p, line).start()
+                for k in range(line):
+                    direct(pass_copy, b, p, k, start)
+
+        product = acc[b]
+        squares = jnp.sum(product * product, axis=0, keepdims=True)
+
+        @pl.when(first)
+        def _():
+            sums[0, b, me] = squares
+            steps(1, n, lambda o: sum_copy(0, b, o, 0).start())
+            steps(0, n, lambda o: sum_copy(0, b, o, 1).start())
+
+        @pl.when(jnp.logical_not(first))
+        def _():
+            sums[1, b, me] = squares
+            steps(1, n, lambda o: sum_copy(1, b, o, 1).start())
+        out_copy(b).start()
+
+    def total_of(kind, b, own):
+        steps(0 if not own else 1, n, lambda o: await_sum(kind, b, lax.rem(me + o, n)))
+        return jnp.sum(sums[kind, b], axis=0)
+
+    @pl.when(first)
+    def _():
+        for b in range(batches):
+            scale = jnp.sqrt(total_of(0, b, True) / (n * rows) + EPS)
+            factor_ref[pl.ds(b, 1), :] = 1.0 / scale
+            log_ref[pl.ds(b, 1), :] = jnp.log(scale)
+
+    @pl.when(jnp.logical_not(first))
+    def _():
+        for b in range(batches):
+            before = jnp.sqrt(total_of(0, b, False) / (n * rows) + EPS)
+            inner = 1.0 / (before * LIFT)
+            scale = jnp.sqrt(total_of(1, b, True) * (inner * inner) / (n * rows) + EPS)
+            factor_ref[pl.ds(b, 1), :] = inner / scale
+            log_ref[pl.ds(b, 1), :] = jnp.log(before) + jnp.log(scale)
+
+    for b in range(batches):
+        out_copy(b).wait()
+        for p in range(pieces):
+            for k in range(1, line):
+                if k > 1 or p < 2:
+                    relay_copy(b, k, p).wait_send()
+            pl.when(inner)(lambda: onward_copy(b, p).wait_send())
+            if p >= 2:
+                swap_copy(b, p).wait_send()
+
+        @pl.when(first)
+        def _():
+            for p in range(pieces):
+                for k in range(line):
+                    direct(own_copy, b, p, k, sent)
+                for k in range(line + 1):
+                    direct(pass_copy, b, p, k, sent)
+            steps(1, n, lambda o: sum_copy(0, b, o, 0).wait_send())
+            steps(0, n, lambda o: sum_copy(0, b, o, 1).wait_send())
+
+        @pl.when(jnp.logical_not(first))
+        def _():
+            steps(1, n, lambda o: sum_copy(1, b, o, 1).wait_send())
+
+
+def pair_call(n, batches, outs, rows, cols):
+    line = n // 2
+    blocks = 2 * n
+    dma = pltpu.SemaphoreType.DMA
+    vmem = pl.BlockSpec(memory_space=pltpu.VMEM)
+    hbm = pl.BlockSpec(memory_space=pltpu.HBM)
+    return pl.pallas_call(
+        functools.partial(pair_kernel, (n, line, batches, outs, rows, cols)),
+        out_shape=(
+            jax.ShapeDtypeStruct((batches, rows, cols), jnp.float32),
+            jax.ShapeDtypeStruct((batches, cols), jnp.float32),
+            jax.ShapeDtypeStruct((batches, cols), jnp.float32),
+        ),
+        in_specs=[vmem, hbm, hbm],
+        out_specs=(hbm, vmem, vmem),
+        scratch_shapes=[
+            pltpu.VMEM((batches, n, rows, cols), jnp.bfloat16),
+            pltpu.VMEM((blocks, rows, outs * rows // 2), jnp.bfloat16),
+            pltpu.VMEM((batches, rows, cols), jnp.float32),
+            pltpu.VMEM((batches, rows, cols), jnp.float32),
+            pltpu.VMEM((batches, rows, cols), jnp.bfloat16),
+            pltpu.VMEM((2, batches, n, 1, cols), jnp.float32),
+            dma((batches,)),
+            dma((blocks, outs)),
+            dma((batches,)),
+            dma((batches, n, 4)),
+            dma((batches, line, 4)),
+            dma((batches, line + 1, 4)),
+            dma((batches, line, 4)),
+            dma((batches, 4)),
+            dma((batches, 4)),
+            dma((2, batches, n)),
+            dma((2, batches, n)),
+        ],
+        compiler_params=pltpu.CompilerParams(
+            collective_id=0, has_side_effects=True, vmem_limit_bytes=56 * 2**20),
+    )
+
+
 def side_of(n):
     side = math.isqrt(n // 2) if n > 1 else 1
     return side if side > 0 and n % side == 0 else 1
@@ -364,6 +678,9 @@
     pieces = 2 if rows % 32 == 0 and rows >= 128 else 1
     per_chunk = 1 if rows % 128 == 0 else side
     n_chunks = n // per_chunk
+    if side == 2 and line == 4 and rows % 256 == 0:
+        prod, factor, logs = pair_call(n, batches, outs, rows, cols)(outcomes[0], environment, tensors[0])
+        return (prod * factor[:, None, :])[None], logs[None]
     dims = (n, line, side, pieces, per_chunk, batches, outs, rows, cols)
     dma = pltpu.SemaphoreType.DMA
     vmem = pl.BlockSpec(memory_space=pltpu.VMEM)

time: 78.5 us -> 72.4 us (0.922)
  Pallas kernels: 74.2 us -> 68 us
    pallas_call x1, Pallas kernels: 74.2 us -> 68 us  [shards(): pair_call(n, batches, outs, rows, cols)]
where the time goes in v1:
time: 72.4 us; the launch traced here: 72.1 us
  Pallas kernels  68 us (94%)
  other arithmetic  2.27 us (3%)
  local copies, waits for them, and re-layouts  1.23 us (2%)
    pallas_call x1, Pallas kernels, shards(): pair_call(n, batches, outs, rows, cols)  68 us
    broadcast_in_dim x1, other arithmetic, shards(): return ((prod * factor[:, None, :])[None], logs[None])  2.27 us

profile of v1, /device:TPU:1, one launch (start us, length us, event | category | flops | bytes accessed | tf_op | source)
XLA Modules:
  0.0 72.1 jit_solution(10798650316623696014)
XLA Ops:
  0.6 68.0 %shard_map.50 = (f32[2,512,256]{2,1,0:T(8,128)}, f32[2,256]{1,0:T(2,128)}, f32[2,256]{1,0:T(2,128)}) custom-call(s32[2,256]{1,0:T(2,128)} %bitcast.6, f32[2,512,256]{2,1,0:T(8,128)} %env_ref.1, bf16[4,512,4096]{2,1,0:T(8,128)(2,1)} %bitcast.5), custom_call_target="tpu_custom_call" | custom-call | tf_op jit(solution)/shard_map/pallas_call | solution.py:682
  68.6 2.3 %multiply_bitcast_fusion = f32[1,2,512,256]{3,2,1,0:T(8,128)} fusion(f32[2,512,256]{2,1,0:T(8,128)} %get-tuple-element.5, f32[2,256]{1,0:T(2,128)} %get-tuple-element.6), kind=kLoop, calls=%fused_computation | loop fusion | flops 262144 | bytes 2099200 | tf_op jit(solution)/shard_map/broadcast_in_dim | solution.py:683
  70.9 1.2 %copy.6 = f32[1,2,256]{2,1,0:T(2,128)} copy(f32[1,2,256]{2,1,0:T(2,128)} %bitcast.7) | data formatting | bytes 4096
